TPU v7x, 32 devices: a whole 2x2x4 slice. The times are simulated.
32 devices in a mesh: dp: 8 (over z, core), mp: 4 (over y, x).
Axes of the slice: x: 2, y: 2, z: 4, core: 2. Of those that a mesh axis runs over, the one named last changes fastest.
Arguments:
- student_in: bfloat16 [128, 6144], P(None, 'mp'), may hold values from -6 to 6
- teacher_hidden: bfloat16 [8192, 128], P('dp'), may hold values from -6 to 6
- w_up: bfloat16 [24576, 6144], P('dp', 'mp'), may hold values from -0.078125 to 0.078125
- w_down: bfloat16 [24576, 6144], P('dp', 'mp'), may hold values from -0.0390625 to 0.0390625
- w_proj: bfloat16 [8192, 6144], P('dp', 'mp'), may hold values from -0.0625 to 0.0625
Outputs:
- grad_up: float32 [24576, 6144], P('dp', 'mp')
- grad_down: float32 [24576, 6144], P('dp', 'mp')
- grad_proj: float32 [8192, 6144], P('dp', 'mp')
All inputs are finite; a program needn't handle non-finite values.
Results may differ from a plain program's by a relative error of at most 0.005.
Values may be sent and summed in bfloat16 or wider, within the bound.
No kernel may reach another device: no remote copies, remote signals or barrier semaphores. Data moves between devices by JAX's collectives and lax.ppermute only.
A program may use at most 128 MiB of HBM per device.

v0:
```python
import math
import jax
import jax.numpy as jnp
from jax import lax
from jax.sharding import PartitionSpec as P


def contract_first(left, right):
    return lax.dot_general(
        left, right, (((0,), (0,)), ((), ())), preferred_element_type=jnp.float32
    )


def contract_last(left, right):
    return lax.dot_general(
        left, right, (((1,), (1,)), ((), ())), preferred_element_type=jnp.float32
    )


def body(student_in, teacher_hidden, w_up, w_down, w_proj):
    tokens_all = student_in.shape[0]
    partial_pre = contract_last(w_up, student_in)
    pre = lax.psum(partial_pre, "mp")
    active = jnp.maximum(pre, 0.0)
    hidden = (active * active).astype(jnp.bfloat16)
    student_part = contract_first(hidden, w_down)
    target_part = contract_first(teacher_hidden, w_proj)
    residual = lax.psum_scatter(student_part - target_part, "dp", scatter_dimension=0, tiled=True)
    d_local = (residual * (1.0 / math.sqrt(tokens_all))).astype(jnp.bfloat16)
    piece = lax.all_gather(d_local, "dp", axis=0, tiled=True)
    proj_acc = jnp.zeros(w_proj.shape, jnp.float32)
    down_acc = jnp.dot(hidden, piece, preferred_element_type=jnp.float32)
    proj_acc = proj_acc - jnp.dot(teacher_hidden, piece, preferred_element_type=jnp.float32)
    grad_cols = contract_last(w_down, piece)
    d_hidden = lax.psum(grad_cols, "mp")
    d_pre = (d_hidden * (2.0 * active)).astype(jnp.bfloat16)
    grad_up = jnp.dot(d_pre, student_in, preferred_element_type=jnp.float32)
    return (grad_up, down_acc, proj_acc)


def solution(mesh):
    return jax.shard_map(
        body,
        mesh=mesh,
        in_specs=(P(None, "mp"), P("dp", None), P("dp", "mp"), P("dp", "mp"), P("dp", "mp")),
        out_specs=(P("dp", "mp"), P("dp", "mp"), P("dp", "mp")),
        check_vma=False,
    )
```

profile of v0, /device:TPU:0, one launch (start us, length us, event | category | flops | bytes accessed | tf_op | source)
XLA Modules:
  0.0 216.5 jit_solution(6784596743819639396)
XLA Ops:
  7.2 0.0 copy-start
  7.2 0.0 all-reduce.3.cloned.1.call-start
  7.2 7.6 %fusion.9 = f32[3072,128]{1,0:T(8,128)} fusion(bf16[3072,1536]{1,0:T(8,128)(2,1)} %param.7, bf16[128,1536]{1,0:T(8,128)(2,1)} %param.5), kind=kOutput, calls=%fused_computation.15 | convolution fusion | flops 1207959552 | bytes 11403264 | tf_op jit(solution)/shard_map/dot_general | solution.py:15
  14.8 0.0 all-reduce.3.cloned.1.call-update
  14.8 0.0 copy-start.4
  14.8 0.0 reduce-scatter.2.cloned.1.call-start
  14.9 63.5 %all-reduce.3.cloned.1.call-done = f32[3072,128]{1,0:T(8,128)} async-done(((f32[3072,128]{1,0:T(8,128)}), f32[3072,128]{1,0:T(8,128)}) %all-reduce.3.cloned.1.call-update) | async-done | bytes 1572880 | tf_op jit(solution)/shard_map/psum | solution.py:23
  78.4 5.6 %fusion.4 = f32[128,1536]{1,0:T(8,128)S(1)} fusion(bf16[3072,1536]{1,0:T(8,128)(2,1)} %param.8, f32[3072,128]{1,0:T(8,128)} %all-reduce.3.cloned.1.call-done), kind=kOutput, calls=%fused_computation.9 | convolution fusion | flops 1209139200 | bytes 11796480 | tf_op jit(solution)/shard_map/dot_general | solution.py:9
  84.1 0.0 copy-done
  84.1 0.0 copy-done.4
  84.1 1.5 convolution_subtract_fusion
  85.6 0.0 reduce-scatter.2.cloned.1.call-update
  85.6 0.0 all-reduce.5.cloned.1.call-start
  85.6 31.9 %reduce-scatter.2.cloned.1.call-done = f32[16,1536]{1,0:T(8,128)} async-done(((f32[128,1536]{1,0:T(8,128)}), f32[16,1536]{1,0:T(8,128)}) %reduce-scatter.2.cloned.1.call-update) | async-done | bytes 98320 | tf_op jit(solution)/shard_map/reduce_scatter | solution.py:28
  117.6 0.9 multiply_convert_fusion.5
  118.5 14.5 %all_gather.3 = bf16[128,1536]{1,0:T(8,128)(2,1)S(1)} all-gather(bf16[16,1536]{1,0:T(8,128)(2,1)S(1)} %multiply_convert_fusion.5), channel_id=1, replica_groups=mesh['dp'=8,'mp'=4] {'dp'}, dimensions={0}, use_global_device_ids=true | all-gather | bytes 442368 | tf_op jit(solution)/shard_map/all_gather | solution.py:30
  132.9 7.4 %convolution_bitcast_fusion = f32[3072,128]{1,0:T(8,128)} fusion(bf16[128,1536]{1,0:T(8,128)(2,1)S(1)} %all_gather.3, bf16[3072,1536]{1,0:T(8,128)(2,1)} %param.8), kind=kOutput, calls=%fused_computation.1 | convolution fusion | flops 1207959552 | bytes 11403264 | tf_op jit(solution)/shard_map/dot_general | solution.py:15
  140.4 0.0 all-reduce.5.cloned.1.call-update
  140.4 3.7 %subtract_bitcast_fusion = f32[1024,1536]{0,1:T(8,128)} fusion(bf16[128,1536]{1,0:T(8,128)(2,1)S(1)} %all_gather.3, bf16[1024,128]{1,0:T(8,128)(2,1)S(1)} %copy-done.4), kind=kOutput, calls=%fused_computation | convolution fusion | flops 404226048 | bytes 6946816 | tf_op jit(solution)/shard_map/dot_general | solution.py:33
  144.1 0.0 copy-start.2
  144.1 6.7 %copy.8 = f32[1024,1536]{1,0:T(8,128)} copy(f32[1024,1536]{0,1:T(8,128)} %subtract_bitcast_fusion) | data formatting | bytes 12582912
  150.9 0.0 copy-done.2
  150.9 0.0 copy-start.3
  150.9 8.2 %fusion.3 = f32[3072,1536]{1,0:T(8,128)} fusion(bf16[128,1536]{1,0:T(8,128)(2,1)S(1)} %all_gather.3, f32[3072,128]{1,0:T(8,128)S(1)} %copy-done.2), kind=kOutput, calls=%fused_computation.8 | convolution fusion | flops 1209139200 | bytes 20840448 | tf_op jit(solution)/shard_map/dot_general | solution.py:32
  159.1 40.6 %all-reduce.5.cloned.1.call-done = f32[3072,128]{1,0:T(8,128)} async-done(((f32[3072,128]{1,0:T(8,128)}), f32[3072,128]{1,0:T(8,128)}) %all-reduce.5.cloned.1.call-update) | async-done | bytes 1572880 | tf_op jit(solution)/shard_map/psum | solution.py:35
  199.7 0.0 copy-done.3
  199.7 0.0 copy-start.1
  199.7 10.3 %fusion = f32[3072,1536]{1,0:T(8,128)} fusion(bf16[128,1536]{1,0:T(8,128)(2,1)S(1)} %copy-done.3, f32[3072,128]{1,0:T(8,128)} %all-reduce.5.cloned.1.call-done, f32[3072,128]{1,0:T(8,128)} %all-reduce.3.cloned.1.call-done), kind=kOutput, calls=%fused_computation.5 | convolution fusion | flops 1209532416 | bytes 22413312 | tf_op jit(solution)/shard_map/dot_general | solution.py:37
  210.0 0.0 copy-done.1
Async XLA Ops:
  7.2 76.9 %copy-start = (bf16[1024,1536]{1,0:T(8,128)(2,1)S(1)}, bf16[1024,1536]{1,0:T(8,128)(2,1)}, u32[]{:S(2)}) copy-start(bf16[1024,1536]{1,0:T(8,128)(2,1)} %param.9) | copy-start | bytes 9437188
  7.2 71.3 %all-reduce.3.cloned.1.call-start = ((), (), s32[]{:S(2)}) async-start(), calls=%async_computation.1 | async-start | bytes 3145728 | tf_op jit(solution)/shard_map/psum | solution.py:23
  14.8 69.2 %copy-start.4 = (bf16[1024,128]{1,0:T(8,128)(2,1)S(1)}, bf16[1024,128]{1,0:T(8,128)(2,1)}, u32[]{:S(2)}) copy-start(bf16[1024,128]{1,0:T(8,128)(2,1)} %param.6) | copy-start | bytes 786436
  14.8 102.7 %reduce-scatter.2.cloned.1.call-start = ((), (), s32[]{:S(2)}) async-start(), calls=%async_computation.2 | async-start | bytes 884736 | tf_op jit(solution)/shard_map/reduce_scatter | solution.py:28
  85.6 114.1 %all-reduce.5.cloned.1.call-start = ((), (), s32[]{:S(2)}) async-start(), calls=%async_computation.3 | async-start | bytes 3145728 | tf_op jit(solution)/shard_map/psum | solution.py:35
  144.1 6.7 %copy-start.2 = (f32[3072,128]{1,0:T(8,128)S(1)}, f32[3072,128]{1,0:T(8,128)}, u32[]{:S(2)}) copy-start(f32[3072,128]{1,0:T(8,128)} %all-reduce.3.cloned.1.call-done) | copy-start | bytes 4718596
  150.9 48.8 %copy-start.3 = (bf16[128,1536]{1,0:T(8,128)(2,1)S(1)}, bf16[128,1536]{1,0:T(8,128)(2,1)}, u32[]{:S(2)}) copy-start(bf16[128,1536]{1,0:T(8,128)(2,1)} %param.5) | copy-start | bytes 1179652
  199.7 10.3 %copy-start.1 = (bf16[1024,1536]{1,0:T(8,128)(2,1)S(1)}, bf16[1024,1536]{1,0:T(8,128)(2,1)}, u32[]{:S(2)}) copy-start(bf16[1024,1536]{1,0:T(8,128)(2,1)} %param.9) | copy-start | bytes 9437188
Sparse Core Ops, SparseCore 0:
  15.0 63.4 all-reduce.2
  85.7 31.8 reduce-scatter.1
  140.5 59.1 all-reduce.4
where the time goes:
time: 217 us; the launch traced here: 216 us
  waiting for transfers between devices  136 us (63%)
  matrix products  44.3 us (20%)
  blocking collectives  14.5 us (7%)
  between operations  13.8 us (6%)
  local copies, waits for them, and re-layouts  6.75 us (3%)
    psum x1, waiting for transfers between devices, body(): pre = lax.psum(partial_pre, 'mp')  63.5 us
    psum x1, waiting for transfers between devices, body(): d_hidden = lax.psum(grad_cols, 'mp')  40.6 us
    reduce_scatter x1, waiting for transfers between devices, body(): lax.psum_scatter(student_part - target_part, 'dp', scatter_dimension=0, t...  31.9 us
    dot_general x2, matrix products, contract_last(): lax.dot_general(left, right, (((1,), (1,)), ((), ())), preferred_element_...  15 us
    all_gather x1, blocking collectives, body(): piece = lax.all_gather(d_local, 'dp', axis=0, tiled=True)  14.5 us
    dot_general x1, matrix products, body(): grad_up = jnp.dot(d_pre, student_in, preferred_element_type=jnp.float32)  10.3 us
    dot_general x1, matrix products, body(): down_acc = jnp.dot(hidden, piece, preferred_element_type=jnp.float32)  8.22 us
    dot_general x2, matrix products, contract_first(): lax.dot_general(left, right, (((0,), (0,)), ((), ())), preferred_element_...  7.09 us
  transfers between devices with their start and end apart: 3, of which 3 were waited for; matrix products, arithmetic and copies ran while one was open for 9% of the time, Pallas kernels for 0%

commit v1 on v0

--- a/solution.py
+++ b/solution.py
@@ -20,7 +20,7 @@
 def body(student_in, teacher_hidden, w_up, w_down, w_proj):
     tokens_all = student_in.shape[0]
     partial_pre = contract_last(w_up, student_in)
-    pre = lax.psum(partial_pre, "mp")
+    pre = jnp.sum(lax.all_gather(partial_pre, "mp"), axis=0)
     active = jnp.maximum(pre, 0.0)
     hidden = (active * active).astype(jnp.bfloat16)
     student_part = contract_first(hidden, w_down)

time: 217 us -> 231 us (1.065)
  waiting for transfers between devices: 136 us -> 146 us
  other arithmetic: 0.9 us -> 5.34 us
    all_gather x0 -> x1, waiting for transfers between devices: none -> 72.9 us  [body(): pre = jnp.sum(lax.all_gather(partial_pre, 'mp'), axis=0)]
    psum x1 -> x0, waiting for transfers between devices: 63.5 us -> none  [body(): pre = lax.psum(partial_pre, 'mp')]
    reduce_sum x0 -> x1, other arithmetic: none -> 4.44 us  [body(): pre = jnp.sum(lax.all_gather(partial_pre, 'mp'), axis=0)]
  transfers between devices with their start and end apart: 3 -> 3, of which waited for: 3 -> 3; matrix products, arithmetic and copies ran while one was open for 9% -> 8% of each run, Pallas kernels for 0% -> 0%
where the time goes in v1:
time: 231 us; the launch traced here: 230 us
  waiting for transfers between devices  146 us (63%)
  matrix products  44.3 us (19%)
  blocking collectives  14.5 us (6%)
  between operations  13.8 us (6%)
  local copies, waits for them, and re-layouts  6.82 us (3%)
  other arithmetic  5.34 us (2%)
    all_gather x1, waiting for transfers between devices, body(): pre = jnp.sum(lax.all_gather(partial_pre, 'mp'), axis=0)  72.9 us
    psum x1, waiting for transfers between devices, body(): d_hidden = lax.psum(grad_cols, 'mp')  40.8 us
    reduce_scatter x1, waiting for transfers between devices, body(): lax.psum_scatter(student_part - target_part, 'dp', scatter_dimension=0, t...  31.9 us
    dot_general x2, matrix products, contract_last(): lax.dot_general(left, right, (((1,), (1,)), ((), ())), preferred_element_...  15 us
    all_gather x1, blocking collectives, body(): piece = lax.all_gather(d_local, 'dp', axis=0, tiled=True)  14.5 us
    dot_general x1, matrix products, body(): grad_up = jnp.dot(d_pre, student_in, preferred_element_type=jnp.float32)  10.3 us
    dot_general x1, matrix products, body(): down_acc = jnp.dot(hidden, piece, preferred_element_type=jnp.float32)  8.22 us
    dot_general x2, matrix products, contract_first(): lax.dot_general(left, right, (((0,), (0,)), ((), ())), preferred_element_...  7.12 us
  transfers between devices with their start and end apart: 3, of which 3 were waited for; matrix products, arithmetic and copies ran while one was open for 8% of the time, Pallas kernels for 0%

profile of v1, /device:TPU:0, one launch (start us, length us, event | category | flops | bytes accessed | tf_op | source)
XLA Modules:
  0.0 230.5 jit_solution(11348924547978161862)
XLA Ops:
  7.2 0.0 copy-start
  7.2 0.0 all-gather.3.cloned.1.call-start
  7.2 7.6 %fusion.9 = f32[3072,128]{1,0:T(8,128)} fusion(bf16[3072,1536]{1,0:T(8,128)(2,1)} %param.7, bf16[128,1536]{1,0:T(8,128)(2,1)} %param.5), kind=kOutput, calls=%fused_computation.15 | convolution fusion | flops 1207959552 | bytes 11403264 | tf_op jit(solution)/shard_map/dot_general | solution.py:15
  14.8 0.0 all-gather.3.cloned.1.call-update
  14.8 0.0 reduce-scatter.2.cloned.1.call-start
  14.9 72.9 %all-gather.3.cloned.1.call-done = f32[12288,128]{1,0:T(8,128)} async-done(((f32[3072,128]{1,0:T(8,128)}), f32[12288,128]{1,0:T(8,128)}) %all-gather.3.cloned.1.call-update) | async-done | bytes 6291472 | tf_op jit(solution)/shard_map/all_gather | solution.py:23
  87.7 4.4 %reduce_sum.9 = f32[3072,128]{1,0:T(8,128)} reduce(f32[4,3072,128]{2,1,0:T(8,128)} %bitcast.16, f32[]{:T(128)} %constant.3.clone.1), dimensions={0}, to_apply=%region_0.0 | reduce | flops 1179648 | bytes 7864324 | tf_op jit(solution)/shard_map/reduce_sum | solution.py:23
  92.2 0.0 copy-start.4
  92.2 5.6 %fusion.4 = f32[128,1536]{1,0:T(8,128)S(1)} fusion(bf16[3072,1536]{1,0:T(8,128)(2,1)} %param.8, f32[3072,128]{1,0:T(8,128)} %reduce_sum.9), kind=kOutput, calls=%fused_computation.9 | convolution fusion | flops 1209139200 | bytes 11796480 | tf_op jit(solution)/shard_map/dot_general | solution.py:9
  97.8 0.0 copy-done
  97.8 0.0 copy-done.4
  97.9 1.5 convolution_subtract_fusion
  99.3 0.0 reduce-scatter.2.cloned.1.call-update
  99.4 0.0 all-reduce.2.cloned.1.call-start
  99.4 31.9 %reduce-scatter.2.cloned.1.call-done = f32[16,1536]{1,0:T(8,128)} async-done(((f32[128,1536]{1,0:T(8,128)}), f32[16,1536]{1,0:T(8,128)}) %reduce-scatter.2.cloned.1.call-update) | async-done | bytes 98320 | tf_op jit(solution)/shard_map/reduce_scatter | solution.py:28
  131.4 0.9 multiply_convert_fusion.5
  132.3 14.5 %all_gather.11 = bf16[128,1536]{1,0:T(8,128)(2,1)S(1)} all-gather(bf16[16,1536]{1,0:T(8,128)(2,1)S(1)} %multiply_convert_fusion.5), channel_id=1, replica_groups=mesh['dp'=8,'mp'=4] {'dp'}, dimensions={0}, use_global_device_ids=true | all-gather | bytes 442368 | tf_op jit(solution)/shard_map/all_gather | solution.py:30
  146.7 7.4 %convolution_bitcast_fusion = f32[3072,128]{1,0:T(8,128)} fusion(bf16[128,1536]{1,0:T(8,128)(2,1)S(1)} %all_gather.11, bf16[3072,1536]{1,0:T(8,128)(2,1)} %param.8), kind=kOutput, calls=%fused_computation.1 | convolution fusion | flops 1207959552 | bytes 11403264 | tf_op jit(solution)/shard_map/dot_general | solution.py:15
  154.2 0.0 all-reduce.2.cloned.1.call-update
  154.2 3.7 %subtract_bitcast_fusion = f32[1024,1536]{0,1:T(8,128)} fusion(bf16[128,1536]{1,0:T(8,128)(2,1)S(1)} %all_gather.11, bf16[1024,128]{1,0:T(8,128)(2,1)S(1)} %copy-done.4), kind=kOutput, calls=%fused_computation | convolution fusion | flops 404226048 | bytes 6946816 | tf_op jit(solution)/shard_map/dot_general | solution.py:33
  157.9 0.0 copy-start.2
  157.9 6.8 %copy.8 = f32[1024,1536]{1,0:T(8,128)} copy(f32[1024,1536]{0,1:T(8,128)} %subtract_bitcast_fusion) | data formatting | bytes 12582912
  164.7 0.0 copy-done.2
  164.7 0.0 copy-start.3
  164.7 8.2 %fusion.3 = f32[3072,1536]{1,0:T(8,128)} fusion(bf16[128,1536]{1,0:T(8,128)(2,1)S(1)} %all_gather.11, f32[3072,128]{1,0:T(8,128)S(1)} %copy-done.2), kind=kOutput, calls=%fused_computation.8 | convolution fusion | flops 1209139200 | bytes 20840448 | tf_op jit(solution)/shard_map/dot_general | solution.py:32
  172.9 40.8 %all-reduce.2.cloned.1.call-done = f32[3072,128]{1,0:T(8,128)} async-done(((f32[3072,128]{1,0:T(8,128)}), f32[3072,128]{1,0:T(8,128)}) %all-reduce.2.cloned.1.call-update) | async-done | bytes 1572880 | tf_op jit(solution)/shard_map/psum | solution.py:35
  213.7 0.0 copy-done.3
  213.7 0.0 copy-start.1
  213.7 10.3 %fusion = f32[3072,1536]{1,0:T(8,128)} fusion(bf16[128,1536]{1,0:T(8,128)(2,1)S(1)} %copy-done.3, f32[3072,128]{1,0:T(8,128)} %all-reduce.2.cloned.1.call-done, f32[3072,128]{1,0:T(8,128)} %reduce_sum.9), kind=kOutput, calls=%fused_computation.5 | convolution fusion | flops 1209532416 | bytes 22413312 | tf_op jit(solution)/shard_map/dot_general | solution.py:37
  223.9 0.0 copy-done.1
Async XLA Ops:
  7.2 90.7 %copy-start = (bf16[1024,1536]{1,0:T(8,128)(2,1)S(1)}, bf16[1024,1536]{1,0:T(8,128)(2,1)}, u32[]{:S(2)}) copy-start(bf16[1024,1536]{1,0:T(8,128)(2,1)} %param.9) | copy-start | bytes 9437188
  7.2 80.6 %all-gather.3.cloned.1.call-start = ((), (), s32[]{:S(2)}) async-start(), calls=%async_computation.3 | async-start | bytes 7864320 | tf_op jit(solution)/shard_map/all_gather | solution.py:23
  14.8 116.5 %reduce-scatter.2.cloned.1.call-start = ((), (), s32[]{:S(2)}) async-start(), calls=%async_computation.1 | async-start | bytes 884736 | tf_op jit(solution)/shard_map/reduce_scatter | solution.py:28
  92.2 5.7 %copy-start.4 = (bf16[1024,128]{1,0:T(8,128)(2,1)S(1)}, bf16[1024,128]{1,0:T(8,128)(2,1)}, u32[]{:S(2)}) copy-start(bf16[1024,128]{1,0:T(8,128)(2,1)} %param.6) | copy-start | bytes 786436
  99.4 114.3 %all-reduce.2.cloned.1.call-start = ((), (), s32[]{:S(2)}) async-start(), calls=%async_computation.2 | async-start | bytes 3145728 | tf_op jit(solution)/shard_map/psum | solution.py:35
  157.9 6.8 %copy-start.2 = (f32[3072,128]{1,0:T(8,128)S(1)}, f32[3072,128]{1,0:T(8,128)}, u32[]{:S(2)}) copy-start(f32[3072,128]{1,0:T(8,128)} %reduce_sum.9) | copy-start | bytes 4718596
  164.7 49.0 %copy-start.3 = (bf16[128,1536]{1,0:T(8,128)(2,1)S(1)}, bf16[128,1536]{1,0:T(8,128)(2,1)}, u32[]{:S(2)}) copy-start(bf16[128,1536]{1,0:T(8,128)(2,1)} %param.5) | copy-start | bytes 1179652
  213.7 10.3 %copy-start.1 = (bf16[1024,1536]{1,0:T(8,128)(2,1)S(1)}, bf16[1024,1536]{1,0:T(8,128)(2,1)}, u32[]{:S(2)}) copy-start(bf16[1024,1536]{1,0:T(8,128)(2,1)} %param.9) | copy-start | bytes 9437188
Sparse Core Ops, SparseCore 0:
  15.0 72.7 all-gather.2
  99.5 31.8 reduce-scatter.1
  154.3 59.3 all-reduce.1
